TPU v7x, 768 devices: a whole 4x8x12 slice. The times are simulated.
768 devices in a mesh: grp: 2 (over z_hi), row: 48 (over x, z_lo, core), col: 8 (over y).
Axes of the slice: x: 4, y: 8, z: 12 (z_hi: 2, z_lo: 6; z = z_hi * 6 + z_lo), core: 2. Of those that a mesh axis runs over, the one named last changes fastest.
Arguments:
- right_side: float32 [2, 16, 147456], P(None, None, 'row'), may hold values from -6 to 6
- near_tiles: bfloat16 [2, 6144, 256, 256], P(None, ('grp', 'row', 'col')), may hold values from -0.078125 to 0.078125
- tile_pairs: int32 [6144], P(('grp', 'row', 'col')), may hold values from 0 to 59, as said below
- tile_count: int32 [768], P(('grp', 'row', 'col')), may hold values from 1 to 8, as said below
- panel_expansions: bfloat16 [2, 147456, 441], P(None, 'row'), may hold values from -0.125 to 0.125
- leaf_of_panel: int32 [48, 3072], P('row'), may hold values from 0 to 23, never falling along the last dimension, each value on 1 to 256 neighbouring positions
- far_pick: int32 [48, 48, 2], replicated, may hold values from 0 to 23, as said below
- far_target: int32 [48, 96], P('row'), may hold values from 0 to 23
- far_offset: int32 [48, 96], P('row'), may hold values from 0 to 3
- translations: bfloat16 [4, 2, 441, 441], replicated, may hold values from -0.109375 to 0.109375
Outputs:
- solution: float32 [2, 16, 147456], P(None, None, 'row')
Inputs may be any that keep to these rules, and one draw needn't show every extreme that they name: `tile_pairs`: within one device's 8 slots the codes are distinct, and over the live slots of all devices with the same row index they are distinct too. `tile_count`: some device has all 8 slots live. far_pick[d, r] holds 2 distinct leaves.
All inputs are finite; a program needn't handle non-finite values.
Results may differ from a plain program's by a relative error of at most 0.0016.
Values may be sent and summed in bfloat16 or wider, within the bound.
A program may use at most 64 MiB of HBM per device.

v0:
```python
import jax
import jax.numpy as jnp
from jax import lax
from jax.sharding import PartitionSpec as P

REACH = 2
OFFSETS = 4
LEAF_DEV = 24


EPSILON = 1e-06
HIGHEST = lax.Precision.HIGHEST


def extended_2(array, sides, width):
    for axis, dim in sides:
        count, length = (lax.axis_size(axis), array.shape[dim])
        up = [(i, (i + 1) % count) for i in range(count)]
        down = [(j, i) for i, j in up]
        last = lax.slice_in_dim(array, length - width, length, axis=dim)
        leading = lax.slice_in_dim(array, 0, width, axis=dim)
        before = lax.ppermute(last, axis, up)
        after = lax.ppermute(leading, axis, down)
        array = jnp.concatenate([before, array, after], axis=dim)
    return array


def complex_mix(products):
    return jnp.stack([products[0, 0] - products[1, 1], products[0, 1] + products[1, 0]])


def inner_local(left, right):
    real_part = jnp.sum(left[0] * right[0] + left[1] * right[1], axis=-1)
    imag_part = jnp.sum(left[0] * right[1] - left[1] * right[0], axis=-1)
    return jnp.stack([real_part, imag_part])


def scaled_vector(coeff, vector):
    real_coeff = coeff[0][:, None]
    imag_coeff = coeff[1][:, None]
    return jnp.stack(
        [
            real_coeff * vector[0] - imag_coeff * vector[1],
            real_coeff * vector[1] + imag_coeff * vector[0],
        ]
    )


def complex_times(left, right):
    return jnp.stack(
        [left[0] * right[0] - left[1] * right[1], left[0] * right[1] + left[1] * right[0]]
    )


def conjugate(value):
    return jnp.stack([value[0], -value[1]])


def small_solve(beta_norm, h_first, h_sub, h_upper, h_middle, h_last):
    radius = jnp.sqrt(h_first[0] * h_first[0] + h_first[1] * h_first[1] + h_sub * h_sub)
    cosine = h_first / radius
    sine_one = h_sub / radius
    upper_row = complex_times(conjugate(cosine), h_upper) + sine_one * h_middle
    lower_row = complex_times(cosine, h_middle) - sine_one * h_upper
    radius_two = jnp.sqrt(
        lower_row[0] * lower_row[0] + lower_row[1] * lower_row[1] + h_last * h_last
    )
    cosine_two = lower_row / radius_two
    goal_top = conjugate(cosine) * beta_norm
    goal_mid = -sine_one * beta_norm
    weight_two = conjugate(cosine_two) * (goal_mid / radius_two)
    weight_one = (goal_top - complex_times(upper_row, weight_two)) / radius
    return (weight_one, weight_two)


def row_total(partial_value):
    return lax.psum(partial_value, "row")


def near_part(vector_low, near_tiles, tile_pairs, tile_count):
    fields = vector_low.shape[1]
    panels = vector_low.shape[2]
    tile_size = near_tiles.shape[2]
    blocks_here = panels // tile_size
    span_count = 2 * REACH + 1
    extended = extended_2(vector_low, (("row", 2),), REACH * tile_size)
    blocks = extended.reshape(2, fields, blocks_here + 2 * REACH, tile_size)
    target = tile_pairs // span_count
    source = target + tile_pairs % span_count
    source_rows = jnp.take(blocks, source, axis=2)
    values = complex_mix(
        jnp.einsum("xstj,ytij->xysti", source_rows, near_tiles, preferred_element_type=jnp.float32)
    )
    live_mask = (jnp.arange(tile_pairs.shape[0], dtype=jnp.int32) < tile_count[0]).astype(
        jnp.float32
    )
    placing = (target[:, None] == jnp.arange(blocks_here, dtype=jnp.int32)[None, :]).astype(
        jnp.float32
    ) * live_mask[:, None]
    summed = jnp.einsum("xsti,tb->xsbi", values, placing, precision=HIGHEST)
    return summed.reshape(2, fields, panels)


def local(
    right_side,
    near_tiles,
    tile_pairs,
    tile_count,
    panel_expansions,
    leaf_of_panel,
    far_pick,
    far_target,
    far_offset,
    translations,
):
    fields = right_side.shape[1]
    coefs = panel_expansions.shape[2]
    share_count = fields // (lax.axis_size("grp") * lax.axis_size("col"))
    own_index = lax.axis_index("grp") * lax.axis_size("col") + lax.axis_index("col")
    row_here = lax.axis_index("row")
    row_count = lax.axis_size("row")
    leaf_ids = jnp.arange(LEAF_DEV, dtype=jnp.int32)
    member_lp = (leaf_of_panel[0][None, :] == leaf_ids[:, None]).astype(jnp.bfloat16)
    member_wide = (leaf_of_panel[0][:, None] == leaf_ids[None, :]).astype(jnp.float32)
    item_keys = far_offset[0] * LEAF_DEV + far_target[0]
    selector = (
        jnp.arange(OFFSETS * LEAF_DEV, dtype=jnp.int32)[:, None] == item_keys[None, :]
    ).astype(jnp.bfloat16)

    def translate(gathered):
        rows_now = gathered.shape[1]
        gathered_low = gathered.astype(jnp.bfloat16).reshape(2, rows_now, OFFSETS, LEAF_DEV, coefs)
        local_field = complex_mix(
            jnp.einsum(
                "xsolk,oykj->xyslj", gathered_low, translations, preferred_element_type=jnp.float32
            )
        )
        return local_field.astype(jnp.bfloat16)

    def far_part(vector_mine):
        weighted = member_lp[None, None] * vector_mine[:, :, None, :]
        multipoles = complex_mix(
            jnp.einsum(
                "xslp,ypk->xyslk", weighted, panel_expansions, preferred_element_type=jnp.float32
            )
        ).astype(jnp.bfloat16)
        pick_codes = lax.dynamic_index_in_dim(far_pick, row_here, 0, keepdims=False)
        chosen = (jnp.arange(row_count, dtype=jnp.int32)[:, None] * LEAF_DEV + pick_codes).reshape(
            -1
        )
        piece = lax.all_gather(multipoles, "row", axis=2, tiled=True)
        piece_count = piece.shape[2]
        hit_table = (chosen[:, None] == jnp.arange(piece_count, dtype=jnp.int32)[None, :]).astype(
            jnp.bfloat16
        )
        weights = jnp.dot(selector, hit_table, preferred_element_type=jnp.float32).astype(
            jnp.bfloat16
        )
        gathered = jnp.einsum("an,xsnk->xsak", weights, piece, preferred_element_type=jnp.float32)
        local_field = translate(gathered)
        per_leaf = jnp.einsum(
            "ypk,xslk->xyspl", panel_expansions, local_field, preferred_element_type=jnp.float32
        )
        picked = jnp.sum(per_leaf * member_wide[None, None, None], axis=-1)
        return complex_mix(picked)

    def apply_operator(vector):
        vector_low = vector.astype(jnp.bfloat16)
        near_image = near_part(vector_low, near_tiles, tile_pairs, tile_count)
        vector_mine = lax.dynamic_slice_in_dim(vector_low, own_index * share_count, share_count, 1)
        far_image = far_part(vector_mine)
        near_all = lax.psum(near_image, ("grp", "col"))
        far_all = lax.all_gather(far_image, ("grp", "col"), axis=1, tiled=True)
        return 0.5 * vector + near_all + far_all

    beta_norm = jnp.sqrt(row_total(jnp.sum(right_side * right_side, axis=(0, 2))) + EPSILON)
    first_basis = right_side / beta_norm[None, :, None]
    image_one = apply_operator(first_basis)
    h_first = row_total(inner_local(first_basis, image_one))
    residue = image_one - scaled_vector(h_first, first_basis)
    h_sub = jnp.sqrt(row_total(jnp.sum(residue * residue, axis=(0, 2))) + EPSILON)
    second_basis = residue / h_sub[None, :, None]
    image_two = apply_operator(second_basis)
    both_products = row_total(
        jnp.stack([inner_local(first_basis, image_two), inner_local(second_basis, image_two)])
    )
    h_upper = both_products[0]
    h_middle = both_products[1]
    remainder = (
        image_two - scaled_vector(h_upper, first_basis) - scaled_vector(h_middle, second_basis)
    )
    h_last = jnp.sqrt(row_total(jnp.sum(remainder * remainder, axis=(0, 2))) + EPSILON)
    weight_one, weight_two = small_solve(beta_norm, h_first, h_sub, h_upper, h_middle, h_last)
    return scaled_vector(weight_one, first_basis) + scaled_vector(weight_two, second_basis)


def solution(mesh):
    return jax.shard_map(
        local,
        mesh=mesh,
        in_specs=(
            P(None, None, "row"),
            P(None, ("grp", "row", "col"), None, None),
            P(("grp", "row", "col")),
            P(("grp", "row", "col")),
            P(None, "row", None),
            P("row", None),
            P(),
            P("row", None),
            P("row", None),
            P(),
        ),
        out_specs=P(None, None, "row"),
        check_vma=False,
    )
```

profile of v0, /device:TPU:1, one launch (start us, length us, event | category | flops | bytes accessed | tf_op | source)
XLA Modules:
  0.0 1236.6 jit_solution(521307866479678054)
XLA Ops:
  7.4 1.3 multiply_reduce_fusion.1
  8.7 146.4 %psum.49 = f32[16]{0:T(128)S(1)} all-reduce(f32[16]{0:T(128)S(1)} %multiply_reduce_fusion.1), channel_id=1, replica_groups=mesh['grp'=2,'row'=48,'col'=8] {'row'}, use_global_device_ids=true, to_apply=%region_1.0 | all-reduce | flops 16 | bytes 128 | tf_op jit(solution)/shard_map/psum | solution.py:77
  155.8 1.2 fusion.143
  157.1 4.3 fusion.6
  162.2 1.9 collective-permute-start
  164.1 6.0 collective-permute-start.1
  174.5 0.8 reshape.796
  175.4 86.7 %all-gather.3.cloned.1.call-done = bf16[2,1,1152,441]{3,2,1,0:T(8,128)(2,1)} async-done(((bf16[2,1,24,441]{3,2,1,0:T(8,128)(2,1)}), bf16[2,1,1152,441]{3,2,1,0:T(8,128)(2,1)}) %all-gather.3.cloned.1.call-update) | async-done | bytes 2032144 | tf_op jit(solution)/shard_map/all_gather | solution.py:151
  262.1 2.2 fusion.51
  264.3 2.8 fusion.14
  267.1 4.5 fusion.45
  271.6 57.8 %all_gather.13 = f32[2,16,3072]{2,0,1:T(2,128)S(1)} all-gather(f32[2,1,3072]{2,0,1:T(2,128)S(1)} %pad_maximum_fusion.6), channel_id=1, replica_groups=mesh['grp'=2,'row'=48,'col'=8] {'grp','col'}, dimensions={1}, use_global_device_ids=true | all-gather | bytes 417792 | tf_op jit(solution)/shard_map/all_gather | solution.py:173
  329.4 79.1 %all-reduce.3.cloned.1.call-done = f32[2,16,3072]{2,1,0:T(8,128)} async-done(((f32[2,16,3072]{2,1,0:T(8,128)}), f32[2,16,3072]{2,1,0:T(8,128)}) %all-reduce.3.cloned.1.call-update) | async-done | bytes 393232 | tf_op jit(solution)/shard_map/psum | solution.py:172
  408.5 1.2 copy_add_fusion.1
  409.8 147.9 %psum.51 = f32[2,16]{1,0:T(2,128)S(1)} all-reduce(f32[2,16]{1,0:T(2,128)S(1)} %pad_maximum_fusion.9), channel_id=1, replica_groups=mesh['grp'=2,'row'=48,'col'=8] {'row'}, use_global_device_ids=true, to_apply=%region_6.8 | all-reduce | flops 32 | bytes 256 | tf_op jit(solution)/shard_map/psum | solution.py:77
  558.7 136.6 %psum.52 = f32[16]{0:T(128)S(1)} all-reduce(f32[16]{0:T(128)S(1)} %multiply_reduce_fusion), channel_id=1, replica_groups=mesh['grp'=2,'row'=48,'col'=8] {'row'}, use_global_device_ids=true, to_apply=%region_8.10 | all-reduce | flops 16 | bytes 128 | tf_op jit(solution)/shard_map/psum | solution.py:77
  695.3 1.1 fusion.142
  697.1 4.4 fusion.2
  702.3 1.9 collective-permute-start.2
  704.2 2.6 collective-permute-start.3
  706.9 2.6 collective-permute-done.3
  711.6 0.8 reshape.800
  712.4 82.5 %all-gather.5.cloned.1.call-done = bf16[2,1,1152,441]{3,2,1,0:T(8,128)(2,1)} async-done(((bf16[2,1,24,441]{3,2,1,0:T(8,128)(2,1)}), bf16[2,1,1152,441]{3,2,1,0:T(8,128)(2,1)}) %all-gather.5.cloned.1.call-update) | async-done | bytes 2032144 | tf_op jit(solution)/shard_map/all_gather | solution.py:151
  794.9 2.2 fusion.54
  797.1 2.8 fusion.12
  799.9 4.5 fusion.48
  804.5 60.8 %all_gather.15 = f32[2,16,3072]{2,0,1:T(2,128)} all-gather(f32[2,1,3072]{2,0,1:T(2,128)S(1)} %pad_maximum_fusion.7), channel_id=1, replica_groups=mesh['grp'=2,'row'=48,'col'=8] {'grp','col'}, dimensions={1}, use_global_device_ids=true | all-gather | bytes 417792 | tf_op jit(solution)/shard_map/all_gather | solution.py:173
  865.3 76.9 %all-reduce.5.cloned.1.call-done = f32[2,16,3072]{2,1,0:T(8,128)} async-done(((f32[2,16,3072]{2,1,0:T(8,128)}), f32[2,16,3072]{2,1,0:T(8,128)}) %all-reduce.5.cloned.1.call-update) | async-done | bytes 393232 | tf_op jit(solution)/shard_map/psum | solution.py:172
  942.2 1.3 copy_add_fusion
  943.8 147.2 %psum.54 = f32[2,2,16]{2,1,0:T(2,128)S(1)} all-reduce(f32[2,2,16]{2,1,0:T(2,128)S(1)} %pad_maximum_fusion.8), channel_id=1, replica_groups=mesh['grp'=2,'row'=48,'col'=8] {'row'}, use_global_device_ids=true, to_apply=%region_15.17 | all-reduce | flops 64 | bytes 512 | tf_op jit(solution)/shard_map/psum | solution.py:77
  1091.5 136.5 %psum.55 = f32[16]{0:T(128)S(1)} all-reduce(f32[16]{0:T(128)S(1)} %fusion.59), channel_id=1, replica_groups=mesh['grp'=2,'row'=48,'col'=8] {'row'}, use_global_device_ids=true, to_apply=%region_17.19 | all-reduce | flops 16 | bytes 128 | tf_op jit(solution)/shard_map/psum | solution.py:77
  1228.3 0.8 maximum_add_fusion
  (111 shorter events, 11.0 us)
Async XLA Ops:
  7.4 165.6 %copy-start = (bf16[2,8,256,256]{3,2,1,0:T(8,128)(2,1)S(1)}, bf16[2,8,256,256]{3,2,1,0:T(8,128)(2,1)}, u32[]{:S(2)}) copy-start(bf16[2,8,256,256]{3,2,1,0:T(8,128)(2,1)} %param.13) | copy-start | bytes 6291460
  7.4 254.7 %all-gather.3.cloned.1.call-start = ((), (), s32[]{:S(2)}) async-start(), calls=%async_computation.1 | async-start | bytes 2408448 | tf_op jit(solution)/shard_map/all_gather | solution.py:151
  155.8 5.6 copy-start.7
  157.1 14.8 %copy-start.10 = (s32[1,96]{1,0:T(1,128)S(1)}, s32[1,96]{1,0:T(1,128)}, u32[]{:S(2)}) copy-start(s32[1,96]{1,0:T(1,128)} %param.19) | copy-start | bytes 1156
  157.1 14.8 %copy-start.11 = (s32[1,96]{1,0:T(1,128)S(1)}, s32[1,96]{1,0:T(1,128)}, u32[]{:S(2)}) copy-start(s32[1,96]{1,0:T(1,128)} %param.20) | copy-start | bytes 1156
  157.1 15.1 %copy-start.9 = (s32[8]{0:T(128)S(1)}, s32[8]{0:T(128)}, u32[]{:S(2)}) copy-start(s32[8]{0:T(128)} %param.14) | copy-start | bytes 100
  157.1 15.1 %copy-start.8 = (s32[1,3072]{1,0:T(1,128)S(1)}, s32[1,3072]{1,0:T(1,128)}, u32[]{:S(2)}) copy-start(s32[1,3072]{1,0:T(1,128)} %param.17) | copy-start | bytes 36868
  162.1 246.4 %all-reduce.3.cloned.1.call-start = ((), (), s32[]{:S(2)}) async-start(), calls=%async_computation | async-start | bytes 786432 | tf_op jit(solution)/shard_map/psum | solution.py:172
  162.2 10.1 collective-permute-start
  164.1 8.2 collective-permute-start.1
  172.2 89.9 %copy-start.1 = (bf16[96,1152,1]{1,0,2:T(8,128)(2,1)}, bf16[96,1152,1]{1,0,2:T(8,128)(2,1)S(1)}, u32[]{:S(2)}) copy-start(bf16[96,1152,1]{1,0,2:T(8,128)(2,1)S(1)} %fusion.34) | copy-start | bytes 663556
  172.3 94.8 %copy-start.5 = (f32[3072,24]{0,1:T(8,128)}, f32[3072,24]{0,1:T(8,128)S(1)}, u32[]{:S(2)}) copy-start(f32[3072,24]{0,1:T(8,128)S(1)} %fusion.65) | copy-start | bytes 884740
  175.3 619.6 %all-gather.5.cloned.1.call-start = ((), (), s32[]{:S(2)}) async-start(), calls=%async_computation.3 | async-start | bytes 2408448 | tf_op jit(solution)/shard_map/all_gather | solution.py:151
  557.8 0.7 copy-start.2
  696.4 0.7 copy-start.3
  697.1 5.1 copy-start.4
  702.2 240.0 %all-reduce.5.cloned.1.call-start = ((), (), s32[]{:S(2)}) async-start(), calls=%async_computation.2 | async-start | bytes 786432 | tf_op jit(solution)/shard_map/psum | solution.py:172
  702.3 4.6 collective-permute-start.2
  704.2 5.2 collective-permute-start.3
  797.1 2.9 copy-start.6
Sparse Core Ops, SparseCore 0:
  162.2 99.8 all-gather.2
  702.3 92.5 all-gather.4
Sparse Core Ops, SparseCore 1:
  175.4 233.0 all-reduce.2
  712.5 229.7 all-reduce.4
where the time goes:
time: 1240 us
  blocking collectives  833 us (67%)
  waiting for transfers between devices  328 us (26%)
  matrix products  30.6 us (2%)
  between operations  16.2 us (1%)
  starting transfers between devices  12.6 us (1%)
    psum x5, blocking collectives, row_total(): return lax.psum(partial_value, 'row')  715 us
    all_gather x2, waiting for transfers between devices, far_part(): piece = lax.all_gather(multipoles, 'row', axis=2, tiled=True)  169 us
    psum x2, waiting for transfers between devices, apply_operator(): near_all = lax.psum(near_image, ('grp', 'col'))  156 us
    all_gather x2, blocking collectives, apply_operator(): far_all = lax.all_gather(far_image, ('grp', 'col'), axis=1, tiled=True)  119 us
  transfers between devices with their start and end apart: 8, of which 5 were waited for; matrix products, arithmetic and copies ran while one was open for 2% of the time, Pallas kernels for 0%

commit v1 on v0

v1 whole, which is shorter than its diff:
```python
import functools

import jax
import jax.numpy as jnp
from jax import lax
from jax.experimental import pallas as pl
from jax.experimental.pallas import tpu as pltpu
from jax.sharding import PartitionSpec as P

REACH = 2
SPAN = 2 * REACH + 1
OFFSETS = 4
LEAVES = 24
SEND = 2
TILE = 256
LANES = 128
EPSILON = 1e-06
MESH = pl.DeviceIdType.MESH
F32 = jnp.float32
BF16 = jnp.bfloat16


def dot(a, b):
    return jnp.dot(a, b, preferred_element_type=F32)


def dot_nt(a, b):
    return lax.dot_general(a, b, (((1,), (1,)), ((), ())), preferred_element_type=F32)


def iota(shape, dim):
    return lax.broadcasted_iota(jnp.int32, shape, dim)


def one_hot(condition):
    return jnp.where(condition, 1.0, 0.0).astype(BF16)


def c_mul(a, b):
    return (a[0] * b[0] - a[1] * b[1], a[0] * b[1] + a[1] * b[0])


def c_add(a, b):
    return (a[0] + b[0], a[1] + b[1])


def c_scale(a, s):
    return (a[0] * s, a[1] * s)


def c_conj(a):
    return (a[0], -a[1])


def c_square(a):
    return a[0] * a[0] + a[1] * a[1]


def solve(bb, bf, bg, ff, fg, gg):
    beta = jnp.sqrt(bb + EPSILON)
    inv = 1.0 / beta
    inv2 = inv * inv
    bb, ff, gg = bb * inv2, ff * inv2, gg * inv2
    bf, bg, fg = c_scale(bf, inv2), c_scale(bg, inv2), c_scale(fg, inv2)
    h11 = (0.5 * bb + bf[0], bf[1])
    a = (0.5 - h11[0], -h11[1])
    u_square = ff + 2.0 * c_mul(c_conj(a), bf)[0] + c_square(a) * bb
    h21 = jnp.sqrt(jnp.maximum(u_square, 0.0) + EPSILON)
    inv21 = 1.0 / h21
    p = (a[0] + 0.5, a[1])
    q = c_scale(a, 0.5)
    x_b = c_add(c_add(bg, c_mul(p, bf)), c_scale(q, bb))
    x_f = c_add(c_add(fg, c_scale(p, ff)), c_mul(q, c_conj(bf)))
    h12 = c_scale(x_b, inv21)
    h22 = c_scale(c_add(x_f, c_mul(c_conj(a), x_b)), inv21 * inv21)
    p2 = (p[0] - h22[0], p[1] - h22[1])
    ha = c_mul(h22, a)
    q2 = (q[0] - x_b[0] - ha[0], q[1] - x_b[1] - ha[1])
    r_square = (
        gg
        + c_square(p2) * ff
        + c_square(q2) * bb
        + 2.0 * c_mul(p2, c_conj(fg))[0]
        + 2.0 * c_mul(q2, c_conj(bg))[0]
        + 2.0 * c_mul(c_mul(c_conj(p2), q2), c_conj(bf))[0]
    ) * (inv21 * inv21)
    h32 = jnp.sqrt(jnp.maximum(r_square, 0.0) + EPSILON)
    rho1 = jnp.sqrt(c_square(h11) + h21 * h21)
    c1 = c_scale(h11, 1.0 / rho1)
    s1 = h21 / rho1
    r12 = c_add(c_mul(c_conj(c1), h12), c_scale(h22, s1))
    t = c_add(c_mul(c1, h22), c_scale(h12, -s1))
    rho2 = jnp.sqrt(c_square(t) + h32 * h32)
    c2 = c_scale(t, 1.0 / rho2)
    y2 = c_scale(c_conj(c2), -s1 * beta / rho2)
    y1 = c_add(c_scale(c_conj(c1), beta), c_scale(c_mul(r12, y2), -1.0))
    y1 = c_scale(y1, 1.0 / rho1)
    y2 = c_scale(y2, inv21)
    alpha = c_scale(c_add(y1, c_mul(y2, a)), inv)
    return alpha, c_scale(y2, inv)


def kernel(
    sizes,
    pairs,
    count,
    pick,
    leaf,
    target,
    offset,
    rhs_hbm,
    tiles_hbm,
    exps_hbm,
    trans_hbm,
    tail_hbm,
    spread,
    coef,
    rhs,
    tiles,
    exps,
    trans,
    pick_rows,
    pick_sel,
    item_sel,
    weave,
    place,
    source_sel,
    field_sel,
    vec,
    far,
    weighted,
    multi_wide,
    multi,
    multi_out,
    multi_in,
    gathered,
    local,
    woven,
    ext_one,
    src,
    values,
    near_out,
    near_in,
    near_part,
    near_cross,
    halo_out,
    halo_in,
    vec_cross,
    ext_wide,
    ext_out,
    ext_in,
    gram_out,
    gram_in,
    coef_out,
    coef_in,
    load_sem,
    send_sem,
    recv_sem,
    many_send,
    many_recv,
):
    n_grp, n_row, n_col, fields, blocks, slots, coefs = sizes
    grp, row, col = lax.axis_index("grp"), lax.axis_index("row"), lax.axis_index("col")
    other = 1 - grp
    mine = grp * n_col + col
    mates = n_grp * n_col
    up, down = lax.rem(row + 1, n_row), lax.rem(row + n_row - 1, n_row)
    full = blocks + 2 * REACH
    rows = 2 * blocks
    pairs_wide = 2 * coefs
    wide = multi_wide.shape[1]
    strips = wide // LANES
    scope = jax.named_scope

    pltpu.make_async_copy(rhs_hbm, rhs, load_sem.at[0]).start()
    for i in range(rows):
        pltpu.make_async_copy(
            exps_hbm.at[:, :, pl.ds(i * LANES, LANES)], exps.at[i], load_sem.at[1]
        ).start()
    pltpu.make_async_copy(tiles_hbm, tiles, load_sem.at[2]).start()
    parts = trans.shape[0]
    for i in range(parts):
        piece = tail_hbm if i == parts - 1 else trans_hbm.at[:, :, :, pl.ds(i * LANES, LANES)]
        pltpu.make_async_copy(piece, trans.at[i], load_sem.at[3]).start()

    def loaded(ref, sem):
        pltpu.make_async_copy(ref, ref, load_sem.at[sem]).wait()

    barrier = pltpu.get_barrier_semaphore()

    def greet(to):
        pl.semaphore_signal(barrier, inc=1, device_id=to, device_id_type=MESH)

    def greet_row(k, carry):
        greet((grp, lax.rem(row + k, n_row), col))
        return carry

    def greet_mate(k, carry):
        mate = lax.rem(mine + k, mates)
        greet((mate // n_col, row, lax.rem(mate, n_col)))
        return carry

    with scope("greet"):
        lax.fori_loop(1, n_row, greet_row, 0)
        lax.fori_loop(1, mates, greet_mate, 0)
        greet((other, up, col))
        greet((other, down, col))

    def send(source, target, sem, to):
        copy = pltpu.make_async_remote_copy(
            src_ref=source,
            dst_ref=target,
            send_sem=send_sem.at[sem],
            recv_sem=recv_sem.at[sem],
            device_id=to,
            device_id_type=MESH,
        )
        copy.start()
        return copy

    def send_many(source, target, sem, to):
        pltpu.make_async_remote_copy(
            src_ref=source,
            dst_ref=target,
            send_sem=many_send.at[sem],
            recv_sem=many_recv.at[sem],
            device_id=to,
            device_id_type=MESH,
        ).start()

    def await_many(ref, sem):
        pltpu.make_async_copy(ref, ref, many_recv.at[sem]).wait()

    def await_sent(ref, sem):
        pltpu.make_async_copy(ref, ref, many_send.at[sem]).wait()

    with scope("right_side"):
        loaded(rhs, 0)
        for x in range(2):
            for b in range(blocks):
                vec[0, x * blocks + b : x * blocks + b + 1, :] = rhs[
                    x, pl.ds(mine, 1), b * TILE : (b + 1) * TILE
                ]
        for b in range(blocks):
            for x in range(2):
                ext_one[b, x * fields : (x + 1) * fields, :] = rhs[
                    x, :, b * TILE : (b + 1) * TILE
                ].astype(BF16)

    def member(b):
        return iota((LEAVES, TILE), 0) == leaf[:, b * TILE : (b + 1) * TILE]

    def weigh(step):
        for b in range(blocks):
            inside = member(b)
            for x in range(2):
                line = vec[step, x * blocks + b : x * blocks + b + 1, :]
                weighted[x * LEAVES : (x + 1) * LEAVES, b * TILE : (b + 1) * TILE] = jnp.where(
                    inside, line, 0.0
                ).astype(BF16)

    with scope("pick_table"):
        multi_wide[...] = jnp.zeros_like(multi_wide)
        multi[...] = jnp.zeros_like(multi)
        halo_out[...] = jnp.zeros_like(halo_out)
        here_lane = iota(pick.shape, 2) == row
        chosen = jnp.sum(jnp.where(here_lane, pick[...].astype(F32), 0.0), axis=2, keepdims=True)
        pick_rows[...] = jnp.broadcast_to(chosen, pick_rows.shape)
        rows16, lanes16 = iota((16, LANES), 0), iota((16, LANES), 1)
        even16 = lax.rem(rows16, 2) == 0
        base16 = jnp.where(rows16 < 2 * strips, (rows16 // 2) * LEAVES, 2 * TILE)

        def build_pick(d, carry):
            own = pick_rows[d].astype(jnp.int32)
            hit = base16 + jnp.where(even16, own[0:1], own[1:2])
            at = pl.ds(pl.multiple_of(d * 16, 16), 16)
            pick_sel[at, 0:LANES] = one_hot(lanes16 == hit)
            pick_sel[at, LANES:] = one_hot(lanes16 + LANES == hit)
            return carry

        lax.fori_loop(0, n_row, build_pick, 0)
    with scope("weigh"):
        weigh(0)
    panels_of = exps.reshape(rows, pairs_wide, LANES)

    def panel_block(b):
        return jnp.concatenate([panels_of[2 * b], panels_of[2 * b + 1]], axis=1)

    def swapped(value):
        left = pltpu.roll(value, wide - 1, 1)
        right = pltpu.roll(value, 1, 1)
        return left, right

    lane_even = lax.rem(iota((LEAVES, wide), 1), 2) == 0

    def far_send(step):
        with scope("multi"):
            every = jnp.concatenate([panel_block(b) for b in range(blocks)], axis=1)
            multi_wide[:, 0:pairs_wide] = dot_nt(weighted[...], every)
            left, right = swapped(multi_wide[LEAVES:, :])
            total = multi_wide[0:LEAVES, :] + jnp.where(lane_even, -left, right)
            for i in range(strips):
                multi[i * LEAVES : (i + 1) * LEAVES, :] = total[:, i * LANES : (i + 1) * LANES]
            multi_out[step] = dot(pick_sel[...], multi[...].astype(BF16)).astype(BF16)
            here = pl.ds(pl.multiple_of(row * 16, 16), 16)
            multi_in[step, here, :] = multi_out[step, here, :]

        def post(k, carry):
            to = lax.rem(row + k, n_row)
            send_many(
                multi_out.at[step, pl.ds(pl.multiple_of(to * 16, 16), 16)],
                multi_in.at[step, here],
                step,
                (grp, to, col),
            )
            return carry

        with scope("multi_send"):
            lax.fori_loop(1, n_row, post, 0)

    def split(value):
        high = value.astype(BF16)
        return high, (value - high.astype(F32)).astype(BF16)

    def far_local(step):
        with scope("multi_wait"):
            await_many(multi_in.at[step, pl.ds(0, (n_row - 1) * 16)], step)
        if step == 0:
            loaded(trans, 3)
        with scope("translate"):
            picked = dot(item_sel[...], multi_in[step])
            pieces = trans.reshape(parts, OFFSETS, pairs_wide, LANES)
            total = None
            for o in range(OFFSETS):
                lines = jnp.concatenate(
                    [
                        picked[(i * OFFSETS + o) * LEAVES : (i * OFFSETS + o + 1) * LEAVES]
                        for i in range(strips)
                    ],
                    axis=1,
                )
                left, right = swapped(lines)
                for x, value in enumerate(
                    (jnp.where(lane_even, lines, -lines), jnp.where(lane_even, left, right))
                ):
                    local[x * LEAVES : (x + 1) * LEAVES, :] = value
                high, low = split(local[...])
                gathered[0 : 2 * LEAVES, :] = high
                gathered[2 * LEAVES :, :] = low
                matrix = jnp.concatenate([pieces[i, o] for i in range(parts)], axis=1)
                term = dot(gathered[:, 0:pairs_wide], matrix)
                total = term if total is None else total + term
            field = total[0 : 2 * LEAVES] + total[2 * LEAVES :]
            real, imag = field[0:LEAVES], field[LEAVES:]
            stacked = []
            for i in range(parts):
                r, m = (v[:, i * LANES : (i + 1) * LANES] for v in (real, imag))
                lines = jnp.concatenate(
                    [jnp.concatenate([r, -m], axis=1), jnp.concatenate([m, r], axis=1)], axis=0
                )
                stacked.extend(split(lines))
            mixed = dot(jnp.concatenate(stacked, axis=0), weave[...]).astype(BF16)
            for i in range(parts):
                woven[:, i * TILE : (i + 1) * TILE] = mixed[
                    i * 4 * LEAVES : (i + 1) * 4 * LEAVES
                ]

    def far_image():
        with scope("evaluate"):
            lines = woven[:, 0:pairs_wide]
            for b in range(blocks):
                found = dot(lines, panel_block(b))
                found = found[0 : 2 * LEAVES] + found[2 * LEAVES :]
                inside = member(b)
                for x in range(2):
                    value = jnp.where(inside, found[x * LEAVES : (x + 1) * LEAVES], 0.0)
                    at = x * blocks + b
                    far[at : at + 1, :] = jnp.sum(value, axis=0, keepdims=True)

    with scope("near_table"):
        targets = [pairs[t] // SPAN for t in range(slots)]
        sources = []
        for t in range(slots):
            rel = targets[t] + lax.rem(pairs[t], SPAN) - REACH
            inner = jnp.where(rel >= blocks, rel + REACH, rel)
            sources.append(jnp.where(rel < 0, rel + blocks + REACH, inner))
        half = 2 * slots * fields
        k_iota = iota((1, 2 * half), 1)
        k_slot = lax.rem(k_iota, slots * fields) // fields
        k_field = lax.rem(k_iota, fields)
        k_part = lax.rem(k_iota, half) // (slots * fields)
        k_target = jnp.full_like(k_iota, -1)
        for t in range(slots):
            goal = jnp.where(t < count[0], targets[t], -1)
            k_target = jnp.where(k_slot == t, goal, k_target)
        width = n_grp * rows
        k_row = lax.rem(k_field, n_col) * width + (k_field // n_col) * rows + k_part * blocks
        k_row = jnp.where(k_target < 0, -1, k_row + k_target)
        place[...] = one_hot(iota(place.shape, 0) == k_row)
        e_iota = iota((2 * fields, source_sel.shape[1]), 1)
        e_rows = iota(e_iota.shape, 0)
        e_group = lax.rem(e_iota // (2 * full) + grp, 2)
        e_field = e_group * n_col + e_iota // (4 * full)
        e_own = e_field + lax.rem(e_iota // full, 2) * fields == e_rows
        e_block = lax.rem(e_iota, full)
        for t in range(slots):
            source_sel[t * 2 * fields : (t + 1) * 2 * fields, :] = one_hot(
                e_own & (e_block == sources[t])
            )
        for b in range(blocks):
            field_sel[b * 2 * fields : (b + 1) * 2 * fields, :] = one_hot(e_own & (e_block == b))

    def near_send(step):
        with scope("near"):
            for t in range(slots):
                by_real = dot_nt(src[t], tiles[0, t])
                by_imag = dot_nt(src[t], tiles[1, t])
                real = by_real[0:fields] - by_imag[fields:]
                imag = by_imag[0:fields] + by_real[fields:]
                for x, value in enumerate((real, imag)):
                    start = (x * slots + t) * fields
                    high, low = split(value)
                    values[start : start + fields, :] = high
                    values[half + start : half + start + fields, :] = low
            image = dot(place[...], values[...]).astype(BF16)
            for c in range(n_col):
                near_out[step, c] = image[c * width : (c + 1) * width]
            near_in[step, col] = near_out[step, col]

        def post(k, carry):
            to = lax.rem(col + k, n_col)
            send_many(near_out.at[step, to], near_in.at[step, col], 2 + step, (grp, row, to))
            return carry

        with scope("near_send"):
            lax.fori_loop(1, n_col, post, 0)

    def near_sum(step):
        with scope("near_wait"):
            await_many(near_in.at[step, pl.ds(0, n_col - 1)], 2 + step)
        with scope("near_sum"):
            near_part[step] = jnp.sum(near_in[step].astype(F32), axis=0)
            start = pl.multiple_of(other * rows, 8)
            return send(
                near_part.at[step, pl.ds(start, rows)],
                near_cross.at[step],
                2 + step,
                (other, row, col),
            )

    def image(step, cross):
        with scope("cross_wait"):
            cross.wait_recv()
        start = pl.multiple_of(grp * rows, 8)
        vec[step + 1] = near_part[step, pl.ds(start, rows), :] + near_cross[step] + far[...]

    with scope("barrier_wait"):
        pl.semaphore_wait(barrier, (n_row - 1) + (mates - 1) + 2)
    halo_one = [
        send(ext_one.at[pl.ds(blocks - 2, 2)], ext_one.at[pl.ds(blocks, 2)], 0, (grp, up, col)),
        send(ext_one.at[pl.ds(0, 2)], ext_one.at[pl.ds(blocks + 2, 2)], 1, (grp, down, col)),
    ]

    with scope("exps_wait"):
        loaded(exps, 1)
    far_send(0)
    with scope("halo_wait"):
        loaded(tiles, 2)
        for copy in halo_one:
            copy.wait_recv()
    for t in range(slots):
        src[t] = ext_one[sources[t]]
    near_send(0)
    with scope("item_table"):
        weave[...] = one_hot(
            iota(weave.shape, 1)
            == 2 * lax.rem(iota(weave.shape, 0), LANES) + iota(weave.shape, 0) // LANES
        )
        keys = (offset[...] * LEAVES + target[...]).astype(F32).astype(BF16)
        item = iota((keys.shape[1], 16 * n_row), 0)
        place_at = iota((keys.shape[1], 16 * n_row), 1)
        repeat = one_hot(
            (item // SEND == place_at // 16) & (lax.rem(item, SEND) == lax.rem(place_at, SEND))
        )
        spread_keys = dot(jnp.broadcast_to(keys, (8, keys.shape[1])), repeat)[0:1]
        strip = lax.rem(iota(spread_keys.shape, 1), 16) // SEND
        hits = spread_keys.astype(jnp.int32) + strip * (OFFSETS * LEAVES)
        item_iota = iota((16, 16 * n_row), 0)
        src_rows = item_sel.shape[0]
        for i in range(src_rows // 16):
            item_sel[i * 16 : (i + 1) * 16, :] = one_hot(item_iota + i * 16 == hits)
    far_local(0)
    cross_one = near_sum(0)
    far_image()
    image(0, cross_one)

    with scope("halo_send"):
        vec_send = send(vec.at[1], vec_cross, 4, (other, row, col))
        for x in range(2):
            last = vec[1, x * blocks + blocks - 2 : (x + 1) * blocks, :]
            halo_out[0, x * 2 : x * 2 + 2, :] = last
            halo_out[1, x * 2 : x * 2 + 2, :] = vec[1, x * blocks : x * blocks + 2, :]
        halo_two = [
            send(halo_out.at[0], halo_in.at[0, 0], 5, (grp, up, col)),
            send(halo_out.at[1], halo_in.at[0, 1], 6, (grp, down, col)),
            send(halo_out.at[0], halo_in.at[1, 0], 7, (other, up, col)),
            send(halo_out.at[1], halo_in.at[1, 1], 8, (other, down, col)),
        ]
        weigh(1)
    far_send(1)
    with scope("vec_wait"):
        vec_send.wait_recv()
        for copy in halo_two:
            copy.wait_recv()
    with scope("extend"):
        for f in range(2):
            for x in range(2):
                lines = (vec[1] if f == 0 else vec_cross[...])[x * blocks : (x + 1) * blocks]
                ext_wide[f, x * full : x * full + blocks, :] = lines
                for side in range(2):
                    start = x * full + blocks + 2 * side
                    ext_wide[f, start : start + 2, :] = halo_in[f, side, x * 2 : x * 2 + 2, :]
        for f in range(2):
            ext_out[0, f], ext_out[1, f] = split(ext_wide[f])
        for i in range(2):
            ext_in[i, col] = ext_out[i]

    def post_ext(i):
        def post(k, carry):
            to = lax.rem(col + k, n_col)
            send_many(ext_out.at[i], ext_in.at[i, col], 4 + i, (grp, row, to))
            return carry

        lax.fori_loop(1, n_col, post, 0)

    def blocks_in(i):
        return jnp.concatenate([ext_in[i, c, f] for c in range(n_col) for f in range(2)], axis=0)

    post_ext(0)
    with scope("ext_wait"):
        await_many(ext_in.at[0, pl.ds(0, n_col - 1)], 4)
    with scope("source"):
        chosen_blocks = dot(source_sel[...], blocks_in(0)).astype(BF16)
        for t in range(slots):
            src[t] = chosen_blocks[t * 2 * fields : (t + 1) * 2 * fields]
    near_send(1)
    post_ext(1)
    far_local(1)
    cross_two = near_sum(1)
    far_image()
    image(1, cross_two)

    with scope("gram"):
        lane = iota((1, LANES), 1)
        v = [vec[i] for i in range(3)]
        turned = [
            jnp.concatenate([vec[i, blocks:, :], -vec[i, 0:blocks, :]], axis=0) for i in range(3)
        ]
        products = [
            v[0] * v[0],
            v[0] * v[1],
            v[0] * turned[1],
            v[0] * v[2],
            v[0] * turned[2],
            v[1] * v[1],
            v[1] * v[2],
            v[1] * turned[2],
            v[2] * v[2],
        ]
        packed = jnp.zeros((1, LANES), F32)
        for i, product in enumerate(products):
            total = jnp.sum(jnp.sum(product, axis=0, keepdims=True), axis=1, keepdims=True)
            packed = jnp.where(lane == i, total, packed)
        gram_out[...] = packed
        gram_in[row] = packed

    def post_gram(k, carry):
        send_many(gram_out, gram_in.at[row], 6, (grp, lax.rem(row + k, n_row), col))
        return carry

    with scope("gram_send"):
        lax.fori_loop(1, n_row, post_gram, 0)
    with scope("spread"):
        await_many(ext_in.at[1, pl.ds(0, n_col - 1)], 5)
        all_fields = dot(field_sel[...], blocks_in(0)) + dot(field_sel[...], blocks_in(1))
        for b in range(blocks):
            for x in range(2):
                start = (b * 2 + x) * fields
                spread[x, :, b * TILE : (b + 1) * TILE] = all_fields[start : start + fields]
    with scope("gram_wait"):
        await_many(gram_in.at[pl.ds(0, n_row - 1)], 6)
    with scope("solve"):
        total = jnp.sum(gram_in[...], axis=0)
        g = [jnp.sum(jnp.where(lane == i, total, 0.0), axis=1, keepdims=True) for i in range(9)]
        alpha, gamma = solve(g[0], (g[1], g[2]), (g[3], g[4]), g[5], (g[6], g[7]), g[8])
        packed = jnp.zeros((1, LANES), F32)
        for i, value in enumerate((*alpha, *gamma)):
            packed = jnp.where(lane == i, value, packed)
        coef_out[...] = packed
        coef_in[mine] = packed

    def post_coef(k, carry):
        mate = lax.rem(mine + k, mates)
        to = (mate // n_col, row, lax.rem(mate, n_col))
        send_many(coef_out, coef_in.at[mine], 7, to)
        return carry

    lax.fori_loop(1, mates, post_coef, 0)
    with scope("coef_wait"):
        await_many(coef_in.at[pl.ds(0, mates - 1)], 7)
    for s in range(fields):
        coef[s : s + 1, :] = coef_in[s]

    with scope("sent_wait"):
        for copy in (*halo_one, cross_one, vec_send, *halo_two, cross_two):
            copy.wait_send()
        for step in range(2):
            await_sent(multi_in.at[step, pl.ds(0, (n_row - 1) * 16)], step)
            await_sent(near_in.at[step, pl.ds(0, n_col - 1)], 2 + step)
            await_sent(ext_in.at[step, pl.ds(0, n_col - 1)], 4 + step)
        await_sent(gram_in.at[pl.ds(0, n_row - 1)], 6)
        await_sent(coef_in.at[pl.ds(0, mates - 1)], 7)


def local_part(
    right_side,
    near_tiles,
    tile_pairs,
    tile_count,
    panel_expansions,
    leaf_of_panel,
    far_pick,
    far_target,
    far_offset,
    translations,
):
    n_grp, n_row, n_col = (lax.axis_size(axis) for axis in ("grp", "row", "col"))
    fields, panels = right_side.shape[1:]
    blocks = panels // TILE
    slots = near_tiles.shape[1]
    coefs = panel_expansions.shape[2]
    parts = pl.cdiv(coefs, LANES)
    strips = pl.cdiv(2 * coefs, LANES)
    exps = jnp.transpose(panel_expansions, (2, 0, 1))
    trans = jnp.transpose(translations, (0, 2, 1, 3))
    whole_part = (parts - 1) * LANES
    spare = [(0, 0)] * 3 + [(0, parts * LANES - coefs)]
    tail = jnp.pad(trans[..., whole_part:], spare)
    full = blocks + 2 * REACH
    rows = 2 * blocks
    depth = n_col * 4 * full
    vm = pltpu.VMEM
    scratch = [
        vm(right_side.shape, F32),
        vm(near_tiles.shape, BF16),
        vm((panels // LANES, coefs, 2, LANES), BF16),
        vm((parts, OFFSETS, coefs, 2, LANES), BF16),
        vm((n_row, SEND, LANES), F32),
        vm((16 * n_row, TILE), BF16),
        vm((strips * OFFSETS * LEAVES, 16 * n_row), BF16),
        vm((TILE, TILE), BF16),
        vm((n_col * n_grp * rows, 4 * slots * fields), BF16),
        vm((slots * 2 * fields, depth), BF16),
        vm((blocks * 2 * fields, depth), BF16),
        vm((3, rows, TILE), F32),
        vm((rows, TILE), F32),
        vm((2 * LEAVES, panels), BF16),
        vm((2 * LEAVES, strips * LANES), F32),
        vm((TILE, LANES), F32),
        vm((2, 16 * n_row, LANES), BF16),
        vm((2, 16 * n_row, LANES), BF16),
        vm((4 * LEAVES, strips * LANES), BF16),
        vm((2 * LEAVES, strips * LANES), F32),
        vm((4 * LEAVES, parts * TILE), BF16),
        vm((full, 2 * fields, TILE), BF16),
        vm((slots, 2 * fields, TILE), BF16),
        vm((4 * slots * fields, TILE), BF16),
        vm((2, n_col, n_grp * rows, TILE), BF16),
        vm((2, n_col, n_grp * rows, TILE), BF16),
        vm((2, n_grp * rows, TILE), F32),
        vm((2, rows, TILE), F32),
        vm((2, 8, TILE), F32),
        vm((2, 2, 8, TILE), F32),
        vm((rows, TILE), F32),
        vm((2, 2 * full, TILE), F32),
        vm((2, 2, 2 * full, TILE), BF16),
        vm((2, n_col, 2, 2 * full, TILE), BF16),
        vm((1, LANES), F32),
        vm((n_row, 1, LANES), F32),
        vm((1, LANES), F32),
        vm((n_grp * n_col, 1, LANES), F32),
        pltpu.SemaphoreType.DMA((4,)),
        pltpu.SemaphoreType.DMA((9,)),
        pltpu.SemaphoreType.DMA((9,)),
        pltpu.SemaphoreType.DMA((8,)),
        pltpu.SemaphoreType.DMA((8,)),
    ]
    smem = pl.BlockSpec(memory_space=pltpu.SMEM)
    whole = pl.BlockSpec(memory_space=pltpu.VMEM)
    hbm = pl.BlockSpec(memory_space=pl.ANY)
    sizes = (n_grp, n_row, n_col, fields, blocks, slots, coefs)
    spread, coef = pl.pallas_call(
        functools.partial(kernel, sizes),
        out_shape=[
            jax.ShapeDtypeStruct(right_side.shape, F32),
            jax.ShapeDtypeStruct((fields, LANES), F32),
        ],
        in_specs=[smem, smem, whole, whole, whole, whole, hbm, hbm, hbm, hbm, hbm],
        out_specs=[whole, whole],
        scratch_shapes=scratch,
        compiler_params=pltpu.CompilerParams(
            collective_id=0, has_side_effects=True, vmem_limit_bytes=60 << 20
        ),
    )(
        tile_pairs,
        tile_count,
        jnp.transpose(far_pick, (0, 2, 1)),
        leaf_of_panel,
        far_target,
        far_offset,
        right_side,
        near_tiles,
        exps,
        trans,
        tail,
    )
    c = [coef[:, i : i + 1] for i in range(4)]
    real = c[0] * right_side[0] - c[1] * right_side[1] + c[2] * spread[0] - c[3] * spread[1]
    imag = c[0] * right_side[1] + c[1] * right_side[0] + c[2] * spread[1] + c[3] * spread[0]
    return jnp.stack([real, imag])


def solution(mesh):
    return jax.shard_map(
        local_part,
        mesh=mesh,
        in_specs=(
            P(None, None, "row"),
            P(None, ("grp", "row", "col"), None, None),
            P(("grp", "row", "col")),
            P(("grp", "row", "col")),
            P(None, "row", None),
            P("row", None),
            P(),
            P("row", None),
            P("row", None),
            P(),
        ),
        out_specs=P(None, None, "row"),
        check_vma=False,
    )
```

time: 1240 us -> 98.5 us (0.08)
  blocking collectives: 833 us -> 0 us
  waiting for transfers between devices: 328 us -> 0 us
  Pallas kernels: 0 us -> 90.9 us
  matrix products: 30.6 us -> 0 us
  between operations: 16.2 us -> 0.68 us
  starting transfers between devices: 12.6 us -> 0 us
    psum x5 -> x0, blocking collectives: 715 us -> none  [row_total(): return lax.psum(partial_value, 'row')]
    all_gather x2 -> x0, waiting for transfers between devices: 169 us -> none  [far_part(): piece = lax.all_gather(multipoles, 'row', axis=2, tiled=True)]
    psum x2 -> x0, waiting for transfers between devices: 156 us -> none  [apply_operator(): near_all = lax.psum(near_image, ('grp', 'col'))]
    all_gather x2 -> x0, blocking collectives: 119 us -> none  [apply_operator(): far_all = lax.all_gather(far_image, ('grp', 'col'), axis=1, tiled=True)]
    pallas_call x0 -> x1, Pallas kernels: none -> 90.9 us  [local_part(): pl.pallas_call(functools.partial(kernel, sizes), out_shape=[jax.ShapeDtyp...]
    dot_general x13 -> x0, matrix products: 30.6 us -> none  [the longest x2 8.9 us: far_part(): jnp.einsum('ypk,xslk->xyspl', panel_expansions, local_field, preferred_el...]
    ppermute x4 -> x0, starting transfers between devices: 12.5 us -> none  [the longest x2 8.62 us: extended_2(): after = lax.ppermute(leading, axis, down)]
  transfers between devices with their start and end apart: 8 -> 0, of which waited for: 5 -> 0; matrix products, arithmetic and copies ran while one was open for 2% -> 0% of each run, Pallas kernels for 0% -> 0%
where the time goes in v1:
time: 98.5 us; the launch traced here: 98.2 us
  Pallas kernels  90.9 us (92%)
  local copies, waits for them, and re-layouts  4.72 us (5%)
  other arithmetic  1.96 us (2%)
    pallas_call x1, Pallas kernels, local_part(): pl.pallas_call(functools.partial(kernel, sizes), out_shape=[jax.ShapeDtyp...  90.9 us

profile of v1, /device:TPU:1, one launch (start us, length us, event | category | flops | bytes accessed | tf_op | source)
XLA Modules:
  0.0 98.2 jit_solution(14570834547594570318)
XLA Ops:
  0.0 1.8 %slice.40 = bf16[4,441,2,57]{3,2,1,0:T(2,128)(2,1)S(1)} slice(bf16[4,441,2,441]{3,2,1,0:T(2,128)(2,1)} %bitcast.3), slice={[0:4], [0:441], [0:2], [384:441]} | slice | bytes 804384 | tf_op jit(solution)/shard_map/slice | solution.py:648
  1.8 1.9 %pad.4.tail_hbm = bf16[4,441,2,128]{3,2,1,0:T(2,128)(2,1)} pad(bf16[4,441,2,57]{3,2,1,0:T(2,128)(2,1)S(1)} %slice.40, bf16[]{:T(256)} %constant.2.clone.1), padding=0_0x0_0x0_0x0_71 | pad | bytes 1305362 | tf_op jit(solution)/shard_map/jit(_pad)/pad | solution.py:648
  4.3 0.0 copy-start
  4.3 90.9 %shard_map.100 = (f32[2,16,3072]{2,1,0:T(8,128)}, f32[16,128]{1,0:T(8,128)}) custom-call(s32[8]{0:T(128)} %pairs.1, s32[1]{0:T(128)S(6)} %copy.11.count, s32[48,2,48]{2,1,0:T(2,128)} %bitcast.6, s32[1,3072]{1,0:T(1,128)} %leaf.1, s32[1,96]{1,0:T(1,128)} %target.1, s32[1,96]{1,0:T(1,128)} %offset.1, f32[2,16,3072]{2,1,0:T(8,128)} %rhs_hbm.1, ...), custom_call_target="tpu_custom_call" | custom-call | tf_op jit(solution)/shard_map/pallas_call | solution.py:702
  95.2 1.1 %slice_reduce_fusion.3 = (f32[16]{0:T(128)S(1)}, f32[16]{0:T(128)S(1)}, f32[16]{0:T(128)S(1)}, f32[16]{0:T(128)S(1)}) fusion(f32[16,128]{1,0:T(8,128)} %get-tuple-element.7), kind=kLoop, calls=%fused_computation.6 | loop fusion | bytes 512 | tf_op jit(solution)/shard_map/slice | solution.py:727
  96.2 0.0 copy-done
  96.3 1.2 %multiply_subtract_fusion = (f32[1,16,3072]{2,1,0:T(8,128)S(1)}, f32[1,16,3072]{2,1,0:T(8,128)S(1)}) fusion(f32[2,16,3072]{2,1,0:T(8,128)} %get-tuple-element.8, f32[2,16,3072]{2,1,0:T(8,128)S(1)} %copy-done, f32[16]{0:T(128)S(1)} %get-tuple-element.10, f32[16]{0:T(128)S(1)} %get-tuple-element.11, f32[16]{0:T(128)S(1)} %get-tuple-element.12, ...), kind=kLoop, calls=%fused_computation.2 | loop fusion | flops 688128 | bytes 1179904 | tf_op jit(solution)/shard_map/sub | solution.py:728
  97.4 0.8 pad_maximum_fusion
Async XLA Ops:
  4.3 91.9 %copy-start = (f32[2,16,3072]{2,1,0:T(8,128)S(1)}, f32[2,16,3072]{2,1,0:T(8,128)}, u32[]{:S(2)}) copy-start(f32[2,16,3072]{2,1,0:T(8,128)} %rhs_hbm.1) | copy-start | bytes 1179652

commit v2 on v1

--- a/solution.py
+++ b/solution.py
@@ -113,8 +113,7 @@
     exps_hbm,
     trans_hbm,
     tail_hbm,
-    spread,
-    coef,
+    out,
     rhs,
     tiles,
     exps,
@@ -149,8 +148,12 @@
     ext_wide,
     ext_out,
     ext_in,
+    spread,
+    coef,
     gram_out,
     gram_in,
+    cross_out,
+    cross_in,
     coef_out,
     coef_in,
     load_sem,
@@ -163,7 +166,9 @@
     grp, row, col = lax.axis_index("grp"), lax.axis_index("row"), lax.axis_index("col")
     other = 1 - grp
     mine = grp * n_col + col
-    mates = n_grp * n_col
+    chips, depth_z = n_row // 12, 6
+    along = grp * depth_z + lax.rem(row // 2, depth_z)
+    beside = (row // (2 * depth_z)) * 2 + lax.rem(row, 2)
     up, down = lax.rem(row + 1, n_row), lax.rem(row + n_row - 1, n_row)
     full = blocks + 2 * REACH
     rows = 2 * blocks
@@ -195,14 +200,21 @@
         greet((grp, lax.rem(row + k, n_row), col))
         return carry
 
-    def greet_mate(k, carry):
-        mate = lax.rem(mine + k, mates)
-        greet((mate // n_col, row, lax.rem(mate, n_col)))
+    def greet_col(k, carry):
+        greet((grp, row, lax.rem(col + k, n_col)))
+        return carry
+
+    def row_of(side, z):
+        return (side // 2) * (2 * depth_z) + z * 2 + lax.rem(side, 2)
+
+    def greet_other(z, carry):
+        greet((other, row_of(beside, z), col))
         return carry
 
     with scope("greet"):
         lax.fori_loop(1, n_row, greet_row, 0)
-        lax.fori_loop(1, mates, greet_mate, 0)
+        lax.fori_loop(0, depth_z, greet_other, 0)
+        lax.fori_loop(1, n_col, greet_col, 0)
         greet((other, up, col))
         greet((other, down, col))
 
@@ -293,20 +305,25 @@
 
     lane_even = lax.rem(iota((LEAVES, wide), 1), 2) == 0
 
-    def far_send(step):
+    here = pl.ds(pl.multiple_of(row * 16, 16), 16)
+
+    def far_multi(step):
         with scope("multi"):
-            every = jnp.concatenate([panel_block(b) for b in range(blocks)], axis=1)
-            multi_wide[:, 0:pairs_wide] = dot_nt(weighted[...], every)
+            total = None
+            for b in range(blocks):
+                term = dot_nt(weighted[:, b * TILE : (b + 1) * TILE], panel_block(b))
+                total = term if total is None else total + term
+            multi_wide[:, 0:pairs_wide] = total
             left, right = swapped(multi_wide[LEAVES:, :])
             total = multi_wide[0:LEAVES, :] + jnp.where(lane_even, -left, right)
             for i in range(strips):
                 multi[i * LEAVES : (i + 1) * LEAVES, :] = total[:, i * LANES : (i + 1) * LANES]
             multi_out[step] = dot(pick_sel[...], multi[...].astype(BF16)).astype(BF16)
-            here = pl.ds(pl.multiple_of(row * 16, 16), 16)
             multi_in[step, here, :] = multi_out[step, here, :]
 
+    def far_post(step):
         def post(k, carry):
-            to = lax.rem(row + k, n_row)
+            to = lax.rem(row + 1 + lax.rem(k + n_row // 3, n_row - 1), n_row)
             send_many(
                 multi_out.at[step, pl.ds(pl.multiple_of(to * 16, 16), 16)],
                 multi_in.at[step, here],
@@ -316,7 +333,7 @@
             return carry
 
         with scope("multi_send"):
-            lax.fori_loop(1, n_row, post, 0)
+            lax.fori_loop(0, n_row - 1, post, 0)
 
     def split(value):
         high = value.astype(BF16)
@@ -377,6 +394,61 @@
                     at = x * blocks + b
                     far[at : at + 1, :] = jnp.sum(value, axis=0, keepdims=True)
 
+    def near_send(step):
+        with scope("near"):
+            for t in range(slots):
+                by_real = dot_nt(src[t], tiles[0, t])
+                by_imag = dot_nt(src[t], tiles[1, t])
+                real = by_real[0:fields] - by_imag[fields:]
+                imag = by_imag[0:fields] + by_real[fields:]
+                for x, value in enumerate((real, imag)):
+                    start = (x * slots + t) * fields
+                    high, low = split(value)
+                    values[start : start + fields, :] = high
+                    values[half + start : half + start + fields, :] = low
+            image = dot(place[...], values[...]).astype(BF16)
+            for c in range(n_col):
+                near_out[step, c] = image[c * width : (c + 1) * width]
+            near_in[step, col] = near_out[step, col]
+
+        def post(k, carry):
+            to = lax.rem(col + k, n_col)
+            send_many(near_out.at[step, to], near_in.at[step, col], 2 + step, (grp, row, to))
+            return carry
+
+        with scope("near_send"):
+            lax.fori_loop(1, n_col, post, 0)
+
+    def near_sum(step):
+        with scope("near_wait"):
+            await_many(near_in.at[step, pl.ds(0, n_col - 1)], 2 + step)
+        with scope("near_sum"):
+            near_part[step] = jnp.sum(near_in[step].astype(F32), axis=0)
+            start = pl.multiple_of(other * rows, 8)
+            return send(
+                near_part.at[step, pl.ds(start, rows)],
+                near_cross.at[step],
+                2 + step,
+                (other, row, col),
+            )
+
+    def image(step, cross):
+        with scope("cross_wait"):
+            cross.wait_recv()
+        start = pl.multiple_of(grp * rows, 8)
+        vec[step + 1] = near_part[step, pl.ds(start, rows), :] + near_cross[step] + far[...]
+
+    with scope("exps_wait"):
+        loaded(exps, 1)
+    far_multi(0)
+    with scope("barrier_wait"):
+        pl.semaphore_wait(barrier, (n_row - 1) + depth_z + (n_col - 1) + 2)
+    halo_one = [
+        send(ext_one.at[pl.ds(blocks - 2, 2)], ext_one.at[pl.ds(blocks, 2)], 0, (grp, up, col)),
+        send(ext_one.at[pl.ds(0, 2)], ext_one.at[pl.ds(blocks + 2, 2)], 1, (grp, down, col)),
+    ]
+    far_post(0)
+
     with scope("near_table"):
         targets = [pairs[t] // SPAN for t in range(slots)]
         sources = []
@@ -397,73 +469,6 @@
         k_row = lax.rem(k_field, n_col) * width + (k_field // n_col) * rows + k_part * blocks
         k_row = jnp.where(k_target < 0, -1, k_row + k_target)
         place[...] = one_hot(iota(place.shape, 0) == k_row)
-        e_iota = iota((2 * fields, source_sel.shape[1]), 1)
-        e_rows = iota(e_iota.shape, 0)
-        e_group = lax.rem(e_iota // (2 * full) + grp, 2)
-        e_field = e_group * n_col + e_iota // (4 * full)
-        e_own = e_field + lax.rem(e_iota // full, 2) * fields == e_rows
-        e_block = lax.rem(e_iota, full)
-        for t in range(slots):
-            source_sel[t * 2 * fields : (t + 1) * 2 * fields, :] = one_hot(
-                e_own & (e_block == sources[t])
-            )
-        for b in range(blocks):
-            field_sel[b * 2 * fields : (b + 1) * 2 * fields, :] = one_hot(e_own & (e_block == b))
-
-    def near_send(step):
-        with scope("near"):
-            for t in range(slots):
-                by_real = dot_nt(src[t], tiles[0, t])
-                by_imag = dot_nt(src[t], tiles[1, t])
-                real = by_real[0:fields] - by_imag[fields:]
-                imag = by_imag[0:fields] + by_real[fields:]
-                for x, value in enumerate((real, imag)):
-                    start = (x * slots + t) * fields
-                    high, low = split(value)
-                    values[start : start + fields, :] = high
-                    values[half + start : half + start + fields, :] = low
-            image = dot(place[...], values[...]).astype(BF16)
-            for c in range(n_col):
-                near_out[step, c] = image[c * width : (c + 1) * width]
-            near_in[step, col] = near_out[step, col]
-
-        def post(k, carry):
-            to = lax.rem(col + k, n_col)
-            send_many(near_out.at[step, to], near_in.at[step, col], 2 + step, (grp, row, to))
-            return carry
-
-        with scope("near_send"):
-            lax.fori_loop(1, n_col, post, 0)
-
-    def near_sum(step):
-        with scope("near_wait"):
-            await_many(near_in.at[step, pl.ds(0, n_col - 1)], 2 + step)
-        with scope("near_sum"):
-            near_part[step] = jnp.sum(near_in[step].astype(F32), axis=0)
-            start = pl.multiple_of(other * rows, 8)
-            return send(
-                near_part.at[step, pl.ds(start, rows)],
-                near_cross.at[step],
-                2 + step,
-                (other, row, col),
-            )
-
-    def image(step, cross):
-        with scope("cross_wait"):
-            cross.wait_recv()
-        start = pl.multiple_of(grp * rows, 8)
-        vec[step + 1] = near_part[step, pl.ds(start, rows), :] + near_cross[step] + far[...]
-
-    with scope("barrier_wait"):
-        pl.semaphore_wait(barrier, (n_row - 1) + (mates - 1) + 2)
-    halo_one = [
-        send(ext_one.at[pl.ds(blocks - 2, 2)], ext_one.at[pl.ds(blocks, 2)], 0, (grp, up, col)),
-        send(ext_one.at[pl.ds(0, 2)], ext_one.at[pl.ds(blocks + 2, 2)], 1, (grp, down, col)),
-    ]
-
-    with scope("exps_wait"):
-        loaded(exps, 1)
-    far_send(0)
     with scope("halo_wait"):
         loaded(tiles, 2)
         for copy in halo_one:
@@ -489,8 +494,22 @@
         src_rows = item_sel.shape[0]
         for i in range(src_rows // 16):
             item_sel[i * 16 : (i + 1) * 16, :] = one_hot(item_iota + i * 16 == hits)
+    with scope("source_table"):
+        e_iota = iota((2 * fields, source_sel.shape[1]), 1)
+        e_rows = iota(e_iota.shape, 0)
+        e_group = lax.rem(e_iota // (2 * full) + grp, 2)
+        e_field = e_group * n_col + e_iota // (4 * full)
+        e_own = e_field + lax.rem(e_iota // full, 2) * fields == e_rows
+        e_block = lax.rem(e_iota, full)
+        for t in range(slots):
+            source_sel[t * 2 * fields : (t + 1) * 2 * fields, :] = one_hot(
+                e_own & (e_block == sources[t])
+            )
+        for b in range(blocks):
+            field_sel[b * 2 * fields : (b + 1) * 2 * fields, :] = one_hot(e_own & (e_block == b))
+
+    cross_one = near_sum(0)
     far_local(0)
-    cross_one = near_sum(0)
     far_image()
     image(0, cross_one)
 
@@ -507,7 +526,7 @@
             send(halo_out.at[1], halo_in.at[1, 1], 8, (other, down, col)),
         ]
         weigh(1)
-    far_send(1)
+    far_multi(1)
     with scope("vec_wait"):
         vec_send.wait_recv()
         for copy in halo_two:
@@ -537,6 +556,7 @@
         return jnp.concatenate([ext_in[i, c, f] for c in range(n_col) for f in range(2)], axis=0)
 
     post_ext(0)
+    far_post(1)
     with scope("ext_wait"):
         await_many(ext_in.at[0, pl.ds(0, n_col - 1)], 4)
     with scope("source"):
@@ -572,14 +592,17 @@
             total = jnp.sum(jnp.sum(product, axis=0, keepdims=True), axis=1, keepdims=True)
             packed = jnp.where(lane == i, total, packed)
         gram_out[...] = packed
-        gram_in[row] = packed
+        gram_in[along] = packed
 
     def post_gram(k, carry):
-        send_many(gram_out, gram_in.at[row], 6, (grp, lax.rem(row + k, n_row), col))
+        to = lax.rem(along + k, n_grp * depth_z)
+        place_to = (to // depth_z, row_of(beside, lax.rem(to, depth_z)), col)
+        send_many(gram_out, gram_in.at[along], 6, place_to)
         return carry
 
+    sides = 2 * chips
     with scope("gram_send"):
-        lax.fori_loop(1, n_row, post_gram, 0)
+        lax.fori_loop(1, n_grp * depth_z, post_gram, 0)
     with scope("spread"):
         await_many(ext_in.at[1, pl.ds(0, n_col - 1)], 5)
         all_fields = dot(field_sel[...], blocks_in(0)) + dot(field_sel[...], blocks_in(1))
@@ -588,28 +611,49 @@
                 start = (b * 2 + x) * fields
                 spread[x, :, b * TILE : (b + 1) * TILE] = all_fields[start : start + fields]
     with scope("gram_wait"):
-        await_many(gram_in.at[pl.ds(0, n_row - 1)], 6)
+        await_many(gram_in.at[pl.ds(0, n_grp * depth_z - 1)], 6)
+        for i in range(n_grp):
+            cross_out[i] = jnp.sum(gram_in[i * depth_z : (i + 1) * depth_z], axis=0)
+        cross_in[beside] = cross_out[...]
+
+    def post_cross(k, carry):
+        to = (grp, row_of(lax.rem(beside + k, sides), lax.rem(row // 2, depth_z)), col)
+        send_many(cross_out, cross_in.at[beside], 7, to)
+        return carry
+
+    lax.fori_loop(1, sides, post_cross, 0)
+    with scope("cross_gram_wait"):
+        await_many(cross_in.at[pl.ds(0, sides - 1)], 7)
     with scope("solve"):
-        total = jnp.sum(gram_in[...], axis=0)
+        total = jnp.sum(cross_in[...], axis=0)
+        total = jnp.concatenate([total[0], total[1]], axis=0)
+        lane = iota((2, LANES), 1)
         g = [jnp.sum(jnp.where(lane == i, total, 0.0), axis=1, keepdims=True) for i in range(9)]
         alpha, gamma = solve(g[0], (g[1], g[2]), (g[3], g[4]), g[5], (g[6], g[7]), g[8])
-        packed = jnp.zeros((1, LANES), F32)
+        packed = jnp.zeros((2, LANES), F32)
         for i, value in enumerate((*alpha, *gamma)):
             packed = jnp.where(lane == i, value, packed)
-        coef_out[...] = packed
-        coef_in[mine] = packed
+        for i in range(n_grp):
+            coef_out[i] = packed[i : i + 1]
+        coef_in[col] = coef_out[...]
 
     def post_coef(k, carry):
-        mate = lax.rem(mine + k, mates)
-        to = (mate // n_col, row, lax.rem(mate, n_col))
-        send_many(coef_out, coef_in.at[mine], 7, to)
+        send_many(coef_out, coef_in.at[col], 8, (grp, row, lax.rem(col + k, n_col)))
         return carry
 
-    lax.fori_loop(1, mates, post_coef, 0)
+    lax.fori_loop(1, n_col, post_coef, 0)
     with scope("coef_wait"):
-        await_many(coef_in.at[pl.ds(0, mates - 1)], 7)
-    for s in range(fields):
-        coef[s : s + 1, :] = coef_in[s]
+        await_many(coef_in.at[pl.ds(0, n_col - 1)], 8)
+    with scope("combine"):
+        for i in range(n_grp):
+            for j in range(n_col):
+                coef[i * n_col + j : i * n_col + j + 1, :] = coef_in[j, i]
+        c = [coef[:, i : i + 1] for i in range(4)]
+        for b in range(blocks):
+            at = slice(b * TILE, (b + 1) * TILE)
+            b0, b1, f0, f1 = rhs[0, :, at], rhs[1, :, at], spread[0, :, at], spread[1, :, at]
+            out[0, :, at] = c[0] * b0 - c[1] * b1 + c[2] * f0 - c[3] * f1
+            out[1, :, at] = c[0] * b1 + c[1] * b0 + c[2] * f1 + c[3] * f0
 
     with scope("sent_wait"):
         for copy in (*halo_one, cross_one, vec_send, *halo_two, cross_two):
@@ -618,8 +662,9 @@
             await_sent(multi_in.at[step, pl.ds(0, (n_row - 1) * 16)], step)
             await_sent(near_in.at[step, pl.ds(0, n_col - 1)], 2 + step)
             await_sent(ext_in.at[step, pl.ds(0, n_col - 1)], 4 + step)
-        await_sent(gram_in.at[pl.ds(0, n_row - 1)], 6)
-        await_sent(coef_in.at[pl.ds(0, mates - 1)], 7)
+        await_sent(gram_in.at[pl.ds(0, n_grp * depth_z - 1)], 6)
+        await_sent(cross_in.at[pl.ds(0, sides - 1)], 7)
+        await_sent(coef_in.at[pl.ds(0, n_col - 1)], 8)
 
 
 def local_part(
@@ -644,8 +689,8 @@
     exps = jnp.transpose(panel_expansions, (2, 0, 1))
     trans = jnp.transpose(translations, (0, 2, 1, 3))
     whole_part = (parts - 1) * LANES
-    spare = [(0, 0)] * 3 + [(0, parts * LANES - coefs)]
-    tail = jnp.pad(trans[..., whole_part:], spare)
+    spare = [(0, 0, 0)] * 3 + [(-whole_part, parts * LANES - coefs, 0)]
+    tail = lax.pad(trans, jnp.zeros((), BF16), spare)
     full = blocks + 2 * REACH
     rows = 2 * blocks
     depth = n_col * 4 * full
@@ -685,28 +730,29 @@
         vm((2, 2 * full, TILE), F32),
         vm((2, 2, 2 * full, TILE), BF16),
         vm((2, n_col, 2, 2 * full, TILE), BF16),
+        vm(right_side.shape, F32),
+        vm((fields, LANES), F32),
         vm((1, LANES), F32),
-        vm((n_row, 1, LANES), F32),
-        vm((1, LANES), F32),
-        vm((n_grp * n_col, 1, LANES), F32),
+        vm((n_grp * 6, 1, LANES), F32),
+        vm((n_grp, 1, LANES), F32),
+        vm((n_row // 6, n_grp, 1, LANES), F32),
+        vm((n_grp, 1, LANES), F32),
+        vm((n_col, n_grp, 1, LANES), F32),
         pltpu.SemaphoreType.DMA((4,)),
         pltpu.SemaphoreType.DMA((9,)),
         pltpu.SemaphoreType.DMA((9,)),
-        pltpu.SemaphoreType.DMA((8,)),
-        pltpu.SemaphoreType.DMA((8,)),
+        pltpu.SemaphoreType.DMA((9,)),
+        pltpu.SemaphoreType.DMA((9,)),
     ]
     smem = pl.BlockSpec(memory_space=pltpu.SMEM)
     whole = pl.BlockSpec(memory_space=pltpu.VMEM)
     hbm = pl.BlockSpec(memory_space=pl.ANY)
     sizes = (n_grp, n_row, n_col, fields, blocks, slots, coefs)
-    spread, coef = pl.pallas_call(
+    return pl.pallas_call(
         functools.partial(kernel, sizes),
-        out_shape=[
-            jax.ShapeDtypeStruct(right_side.shape, F32),
-            jax.ShapeDtypeStruct((fields, LANES), F32),
-        ],
+        out_shape=jax.ShapeDtypeStruct(right_side.shape, F32),
         in_specs=[smem, smem, whole, whole, whole, whole, hbm, hbm, hbm, hbm, hbm],
-        out_specs=[whole, whole],
+        out_specs=whole,
         scratch_shapes=scratch,
         compiler_params=pltpu.CompilerParams(
             collective_id=0, has_side_effects=True, vmem_limit_bytes=60 << 20
@@ -724,10 +770,6 @@
         trans,
         tail,
     )
-    c = [coef[:, i : i + 1] for i in range(4)]
-    real = c[0] * right_side[0] - c[1] * right_side[1] + c[2] * spread[0] - c[3] * spread[1]
-    imag = c[0] * right_side[1] + c[1] * right_side[0] + c[2] * spread[1] + c[3] * spread[0]
-    return jnp.stack([real, imag])
 
 
 def solution(mesh):

time: 98.5 us -> 93 us (0.944)
  Pallas kernels: 90.9 us -> 87.3 us
  other arithmetic: 1.96 us -> 0 us
    pallas_call x1, Pallas kernels: 90.9 us -> 87.3 us  [local_part(): pl.pallas_call(functools.partial(kernel, sizes), out_shape=jax.ShapeDtype...]
    slice x2 -> x0, local copies, waits for them, and re-layouts: 2.86 us -> none  [the longest x1 1.79 us: local_part(): tail = jnp.pad(trans[..., whole_part:], spare)]
    unnamed x2 -> x1, local copies, waits for them, and re-layouts: 0.01 us -> 1.77 us
    pad x1, local copies, waits for them, and re-layouts: 1.86 us -> 3.07 us  [local_part(): tail = lax.pad(trans, jnp.zeros((), BF16), spare)]
    sub x1 -> x0, other arithmetic: 1.18 us -> none  [local_part(): c[0] * right_side[0] - c[1] * right_side[1] + c[2] * spread[0]]
where the time goes in v2:
time: 93 us; the launch traced here: 92.8 us
  Pallas kernels  87.3 us (94%)
  local copies, waits for them, and re-layouts  4.83 us (5%)
    pallas_call x1, Pallas kernels, local_part(): pl.pallas_call(functools.partial(kernel, sizes), out_shape=jax.ShapeDtype...  87.3 us
    pad x1, local copies, waits for them, and re-layouts, local_part(): tail = lax.pad(trans, jnp.zeros((), BF16), spare)  3.07 us

profile of v2, /device:TPU:1, one launch (start us, length us, event | category | flops | bytes accessed | tf_op | source)
XLA Modules:
  0.0 92.8 jit_solution(8450144228556829678)
XLA Ops:
  0.7 3.1 %pad_slice_fusion.tail_hbm = bf16[4,441,2,128]{3,2,1,0:T(2,128)(2,1)} fusion(bf16[4,441,2,441]{3,2,1,0:T(2,128)(2,1)} %bitcast.3), kind=kLoop, calls=%fused_computation | loop fusion | bytes 4014864 | tf_op jit(solution)/shard_map/pad | solution.py:693
  3.7 87.3 %shard_map.100 = f32[2,16,3072]{2,1,0:T(8,128)} custom-call(s32[8]{0:T(128)} %pairs.1, s32[1]{0:T(128)S(6)} %copy.12.count, s32[48,2,48]{2,1,0:T(2,128)} %bitcast.6, s32[1,3072]{1,0:T(1,128)} %leaf.1, s32[1,96]{1,0:T(1,128)} %target.1, s32[1,96]{1,0:T(1,128)} %offset.1, f32[2,16,3072]{2,1,0:T(8,128)} %rhs_hbm.1, bf16[2,8,256,256]{3,2,1,0:T(8,128)(2,1)} %tiles_hbm.1, ...), custom_call_target="tpu_custom_call" | custom-call | tf_op jit(solution)/shard_map/pallas_call | solution.py:751
  91.0 1.8 %copy.13 = f32[2,16,3072]{2,1,0:T(8,128)} copy(f32[2,16,3072]{2,1,0:T(8,128)} %shard_map.100) | data formatting | bytes 786432

commit v3 on v2

--- a/solution.py
+++ b/solution.py
@@ -113,7 +113,8 @@
     exps_hbm,
     trans_hbm,
     tail_hbm,
-    out,
+    out_b,
+    out_f,
     rhs,
     tiles,
     exps,
@@ -526,28 +527,22 @@
             send(halo_out.at[1], halo_in.at[1, 1], 8, (other, down, col)),
         ]
         weigh(1)
-    far_multi(1)
-    with scope("vec_wait"):
-        vec_send.wait_recv()
-        for copy in halo_two:
-            copy.wait_recv()
-    with scope("extend"):
-        for f in range(2):
-            for x in range(2):
-                lines = (vec[1] if f == 0 else vec_cross[...])[x * blocks : (x + 1) * blocks]
-                ext_wide[f, x * full : x * full + blocks, :] = lines
-                for side in range(2):
-                    start = x * full + blocks + 2 * side
-                    ext_wide[f, start : start + 2, :] = halo_in[f, side, x * 2 : x * 2 + 2, :]
-        for f in range(2):
-            ext_out[0, f], ext_out[1, f] = split(ext_wide[f])
+
+    def extend(f):
+        for x in range(2):
+            lines = (vec[1] if f == 0 else vec_cross[...])[x * blocks : (x + 1) * blocks]
+            ext_wide[f, x * full : x * full + blocks, :] = lines
+            for side in range(2):
+                start = x * full + blocks + 2 * side
+                ext_wide[f, start : start + 2, :] = halo_in[f, side, x * 2 : x * 2 + 2, :]
+        ext_out[0, f], ext_out[1, f] = split(ext_wide[f])
         for i in range(2):
-            ext_in[i, col] = ext_out[i]
-
-    def post_ext(i):
+            ext_in[i, col, f] = ext_out[i, f]
+
+    def post_ext(i, f):
         def post(k, carry):
             to = lax.rem(col + k, n_col)
-            send_many(ext_out.at[i], ext_in.at[i, col], 4 + i, (grp, row, to))
+            send_many(ext_out.at[i, f], ext_in.at[i, col, f], 4 + i, (grp, row, to))
             return carry
 
         lax.fori_loop(1, n_col, post, 0)
@@ -555,7 +550,18 @@
     def blocks_in(i):
         return jnp.concatenate([ext_in[i, c, f] for c in range(n_col) for f in range(2)], axis=0)
 
-    post_ext(0)
+    with scope("extend_own"):
+        for copy in halo_two[:2]:
+            copy.wait_recv()
+        extend(0)
+        post_ext(0, 0)
+    far_multi(1)
+    with scope("extend_other"):
+        vec_send.wait_recv()
+        for copy in halo_two[2:]:
+            copy.wait_recv()
+        extend(1)
+        post_ext(0, 1)
     far_post(1)
     with scope("ext_wait"):
         await_many(ext_in.at[0, pl.ds(0, n_col - 1)], 4)
@@ -564,9 +570,10 @@
         for t in range(slots):
             src[t] = chosen_blocks[t * 2 * fields : (t + 1) * 2 * fields]
     near_send(1)
-    post_ext(1)
     far_local(1)
     cross_two = near_sum(1)
+    for f in range(2):
+        post_ext(1, f)
     far_image()
     image(1, cross_two)
 
@@ -652,8 +659,10 @@
         for b in range(blocks):
             at = slice(b * TILE, (b + 1) * TILE)
             b0, b1, f0, f1 = rhs[0, :, at], rhs[1, :, at], spread[0, :, at], spread[1, :, at]
-            out[0, :, at] = c[0] * b0 - c[1] * b1 + c[2] * f0 - c[3] * f1
-            out[1, :, at] = c[0] * b1 + c[1] * b0 + c[2] * f1 + c[3] * f0
+            out_b[0, :, at] = c[0] * b0 - c[1] * b1
+            out_b[1, :, at] = c[0] * b1 + c[1] * b0
+            out_f[0, :, at] = c[2] * f0 - c[3] * f1
+            out_f[1, :, at] = c[2] * f1 + c[3] * f0
 
     with scope("sent_wait"):
         for copy in (*halo_one, cross_one, vec_send, *halo_two, cross_two):
@@ -748,11 +757,11 @@
     whole = pl.BlockSpec(memory_space=pltpu.VMEM)
     hbm = pl.BlockSpec(memory_space=pl.ANY)
     sizes = (n_grp, n_row, n_col, fields, blocks, slots, coefs)
-    return pl.pallas_call(
+    out_b, out_f = pl.pallas_call(
         functools.partial(kernel, sizes),
-        out_shape=jax.ShapeDtypeStruct(right_side.shape, F32),
+        out_shape=[jax.ShapeDtypeStruct(right_side.shape, F32)] * 2,
         in_specs=[smem, smem, whole, whole, whole, whole, hbm, hbm, hbm, hbm, hbm],
-        out_specs=whole,
+        out_specs=[whole, whole],
         scratch_shapes=scratch,
         compiler_params=pltpu.CompilerParams(
             collective_id=0, has_side_effects=True, vmem_limit_bytes=60 << 20
@@ -770,6 +779,7 @@
         trans,
         tail,
     )
+    return out_b + out_f
 
 
 def solution(mesh):

time: 93 us -> 88.5 us (0.952)
  Pallas kernels: 87.3 us -> 82.6 us
  other arithmetic: 0 us -> 1.9 us
  local copies, waits for them, and re-layouts: 4.83 us -> 3.07 us
    pallas_call x1, Pallas kernels: 87.3 us -> 82.6 us  [local_part(): pl.pallas_call(functools.partial(kernel, sizes), out_shape=[jax.ShapeDtyp...]
    add x0 -> x1, other arithmetic: none -> 1.9 us  [local_part(): return out_b + out_f]
    unnamed x1 -> x0, local copies, waits for them, and re-layouts: 1.77 us -> none
where the time goes in v3:
time: 88.5 us; the launch traced here: 88.2 us
  Pallas kernels  82.6 us (93%)
  local copies, waits for them, and re-layouts  3.07 us (3%)
  other arithmetic  1.9 us (2%)
    pallas_call x1, Pallas kernels, local_part(): pl.pallas_call(functools.partial(kernel, sizes), out_shape=[jax.ShapeDtyp...  82.6 us
    pad x1, local copies, waits for them, and re-layouts, local_part(): tail = lax.pad(trans, jnp.zeros((), BF16), spare)  3.07 us
    add x1, other arithmetic, local_part(): return out_b + out_f  1.9 us

profile of v3, /device:TPU:1, one launch (start us, length us, event | category | flops | bytes accessed | tf_op | source)
XLA Modules:
  0.0 88.2 jit_solution(4995315778597230483)
XLA Ops:
  0.7 3.1 %pad_slice_fusion.tail_hbm = bf16[4,441,2,128]{3,2,1,0:T(2,128)(2,1)} fusion(bf16[4,441,2,441]{3,2,1,0:T(2,128)(2,1)} %bitcast.3), kind=kLoop, calls=%fused_computation | loop fusion | bytes 4014864 | tf_op jit(solution)/shard_map/pad | solution.py:702
  3.7 82.6 %shard_map.100 = (f32[2,16,3072]{2,1,0:T(8,128)}, f32[2,16,3072]{2,1,0:T(8,128)}) custom-call(s32[8]{0:T(128)} %pairs.1, s32[1]{0:T(128)S(6)} %copy.11.count, s32[48,2,48]{2,1,0:T(2,128)} %bitcast.6, s32[1,3072]{1,0:T(1,128)} %leaf.1, s32[1,96]{1,0:T(1,128)} %target.1, s32[1,96]{1,0:T(1,128)} %offset.1, f32[2,16,3072]{2,1,0:T(8,128)} %rhs_hbm.1, ...), custom_call_target="tpu_custom_call" | custom-call | tf_op jit(solution)/shard_map/pallas_call | solution.py:760
  86.3 1.9 %add.5 = f32[2,16,3072]{2,1,0:T(8,128)} add(f32[2,16,3072]{2,1,0:T(8,128)} %get-tuple-element.7, f32[2,16,3072]{2,1,0:T(8,128)} %get-tuple-element.8) | non-fusion elementwise | flops 98304 | bytes 1179648 | tf_op jit(solution)/shard_map/add | solution.py:782
